TPU v7x, 512 devices: a whole 4x4x16 slice. The times are simulated.
512 devices in a mesh: rep: 16 (over x, z_lo), mp: 32 (over z_hi, y, core).
Axes of the slice: x: 4, y: 4, z: 16 (z_hi: 4, z_lo: 4; z = z_hi * 4 + z_lo), core: 2. Of those that a mesh axis runs over, the one named last changes fastest.
Arguments:
- dense_feats: bfloat16 [65536, 13], P(('rep', 'mp')), may hold values from -6 to 6
- bag_counts: int32 [65536, 32, 64], P('rep', 'mp'), may hold values from 0 to 2
- emb_rows: bfloat16 [32, 64, 256], P('mp'), may hold values from -0.625 to 0.625
- v_emb: bfloat16 [8192, 256], P('mp'), may hold values from -0.0625 to 0.0625
- u_emb: bfloat16 [256, 8192], P(None, 'mp'), may hold values from -0.375 to 0.375
- b_emb: bfloat16 [8192], P('mp'), may hold values from -3 to 3
- v_bot: bfloat16 [256, 256], replicated, may hold values from -0.375 to 0.375
- u_bot: bfloat16 [256, 256], replicated, may hold values from -0.375 to 0.375
- b_bot: bfloat16 [256], replicated, may hold values from -3 to 3
- w_first: bfloat16 [13, 1024], replicated, may hold values from -1.75 to 1.75
- b_first: bfloat16 [1024], replicated, may hold values from -3 to 3
- w_second: bfloat16 [1024, 256], replicated, may hold values from -0.1875 to 0.1875
- b_second: bfloat16 [256], replicated, may hold values from -3 to 3
- cot_cross: bfloat16 [65536, 8192], P(('rep', 'mp')), may hold values from -24 to 24
- cot_bottom: bfloat16 [65536, 256], P(('rep', 'mp')), may hold values from -6 to 6
Outputs:
- cross_emb: bfloat16 [65536, 8192], P(('rep', 'mp'))
- cross_bot: bfloat16 [65536, 256], P(('rep', 'mp'))
- grad_table: bfloat16 [32, 64, 256], P('mp')
- grad_v_emb: bfloat16 [8192, 256], P('mp')
- grad_u_emb: bfloat16 [256, 8192], P(None, 'mp')
- grad_b_emb: bfloat16 [8192], P('mp')
- grad_v_bot: bfloat16 [256, 256], replicated
- grad_u_bot: bfloat16 [256, 256], replicated
- grad_b_bot: bfloat16 [256], replicated
- grad_w_first: bfloat16 [13, 1024], replicated
- grad_b_first: bfloat16 [1024], replicated
- grad_w_second: bfloat16 [1024, 256], replicated
- grad_b_second: bfloat16 [256], replicated
Inputs may be any that keep to these rules, and one draw needn't show every extreme that they name: bag_counts[s, t, j] is how often row j of table t occurs in the bag of sample s.
All inputs are finite; a program needn't handle non-finite values.
Results may differ from a plain program's by a relative error of at most 0.029.
Values may be sent and summed in bfloat16 or wider, within the bound.
A program may use at most 64 MiB of HBM per device.

v0:
```python
import math
import jax
import jax.numpy as jnp
from jax import lax
from jax.sharding import PartitionSpec as P


def silu_slope(inputs):
    gate_value = jax.nn.sigmoid(inputs)
    return gate_value * (1.0 + inputs * (1.0 - gate_value))


def contract_rows(left_side, right_side):
    return lax.dot_general(
        left_side, right_side, (((0,), (0,)), ((), ())), preferred_element_type=jnp.float32
    )


def contract_cols(left_side, right_side):
    return lax.dot_general(
        left_side, right_side, (((1,), (1,)), ((), ())), preferred_element_type=jnp.float32
    )


def local(
    dense_feats,
    bag_counts,
    emb_rows,
    v_emb,
    u_emb,
    b_emb,
    v_bot,
    u_bot,
    b_bot,
    w_first,
    b_first,
    w_second,
    b_second,
    cot_cross,
    cot_bottom,
):
    tables = lax.axis_size("mp")
    replicas = lax.axis_size("rep")
    own_rows = dense_feats.shape[0]
    table_rows, width = emb_rows.shape[1:]
    rank = v_emb.shape[1]
    share = width // replicas
    grad_scale = 1.0 / math.sqrt(own_rows * tables * replicas)
    first = lax.axis_index("rep") * share
    pad = -(table_rows + 1) % 128
    packed = jnp.concatenate(
        [v_emb, u_emb.T, emb_rows[0].T, b_emb[:, None], jnp.zeros((width, pad), jnp.bfloat16)],
        axis=1,
    )
    packed = lax.dynamic_slice_in_dim(packed, first, share, 0)
    columns = packed.shape[1]
    packed = lax.all_gather(packed, "mp", axis=0, tiled=True)
    packed = lax.all_gather(packed, "rep", axis=0, tiled=True)
    packed = jnp.swapaxes(packed.reshape(replicas, tables, share, columns), 0, 1)
    packed = packed.reshape(tables * width, columns)
    counts = bag_counts[:, 0, :].astype(jnp.bfloat16)
    counts = jnp.swapaxes(counts.reshape(tables, own_rows, table_rows), 1, 2)
    counts = lax.all_to_all(counts, "mp", split_axis=0, concat_axis=0, tiled=True)
    first_pre = jnp.dot(dense_feats, w_first, preferred_element_type=jnp.float32) + b_first.astype(
        jnp.float32
    )
    first_act = jax.nn.silu(first_pre).astype(jnp.bfloat16)
    second_pre = jnp.dot(first_act, w_second, preferred_element_type=jnp.float32) + b_second.astype(
        jnp.float32
    )
    bottom = jax.nn.silu(second_pre).astype(jnp.bfloat16)
    v_all = packed[:, :rank]
    u_all = packed[:, rank : 2 * rank]
    emb_all = packed[:, 2 * rank : 2 * rank + table_rows].reshape(tables, width, table_rows)
    b_all = packed[:, 2 * rank + table_rows].reshape(1, tables * width).astype(jnp.float32)
    pooled = lax.dot_general(
        counts, emb_all, (((1,), (2,)), ((0,), (0,))), preferred_element_type=jnp.float32
    ).astype(jnp.bfloat16)
    pooled = jnp.swapaxes(pooled, 0, 1).reshape(own_rows, tables * width)
    low_rank = (
        jnp.dot(pooled, v_all, preferred_element_type=jnp.float32)
        + jnp.dot(bottom, v_bot, preferred_element_type=jnp.float32)
    ).astype(jnp.bfloat16)
    lift_emb = contract_cols(low_rank, u_all) + b_all
    pooled_full = pooled.astype(jnp.float32)
    cross_emb = (pooled_full * (lift_emb + 1.0)).astype(jnp.bfloat16)
    lift_bottom = jnp.dot(low_rank, u_bot, preferred_element_type=jnp.float32) + b_bot.astype(
        jnp.float32
    )
    bottom_full = bottom.astype(jnp.float32)
    cross_bot = (bottom_full * (lift_bottom + 1.0)).astype(jnp.bfloat16)
    cot_rows = cot_cross.astype(jnp.float32)
    d_lift = cot_rows * pooled_full
    d_lift_round = d_lift.astype(jnp.bfloat16)
    cot_low = cot_bottom.astype(jnp.float32)
    d_bottom_lift = cot_low * bottom_full
    d_bottom_round = d_bottom_lift.astype(jnp.bfloat16)
    d_low = (
        jnp.dot(d_lift_round, u_all, preferred_element_type=jnp.float32)
        + contract_cols(d_bottom_round, u_bot)
    ).astype(jnp.bfloat16)
    d_pooled = (cot_rows * (lift_emb + 1.0) + contract_cols(d_low, v_all)).astype(jnp.bfloat16)
    d_tables = jnp.swapaxes(d_pooled.reshape(own_rows, tables, width), 0, 1)
    grad_table = lax.dot_general(
        d_tables, counts, (((1,), (2,)), ((0,), (0,))), preferred_element_type=jnp.float32
    ).reshape(tables * width, table_rows)
    grad_v = contract_rows(pooled, d_low)
    grad_u = contract_rows(d_lift_round, low_rank)
    grad_b = jnp.sum(d_lift, axis=0)
    grads = jnp.concatenate(
        [
            grad_v.astype(jnp.bfloat16),
            grad_u.astype(jnp.bfloat16),
            grad_table.astype(jnp.bfloat16),
            grad_b.astype(jnp.bfloat16)[:, None],
            jnp.zeros((tables * width, pad), jnp.bfloat16),
        ],
        axis=1,
    )
    d_bottom = cot_low * (lift_bottom + 1.0) + contract_cols(d_low, v_bot)
    grad_vb = grad_scale * contract_rows(bottom, d_low)
    grad_ub = grad_scale * contract_rows(low_rank, d_bottom_round)
    grad_bb = grad_scale * jnp.sum(d_bottom_lift, axis=0)
    d_second = d_bottom * silu_slope(second_pre)
    d_second_round = d_second.astype(jnp.bfloat16)
    grad_ws = grad_scale * contract_rows(first_act, d_second_round)
    grad_bs = grad_scale * jnp.sum(d_second, axis=0)
    d_first = contract_cols(d_second_round, w_second) * silu_slope(first_pre)
    d_first_round = d_first.astype(jnp.bfloat16)
    grad_wf = grad_scale * contract_rows(dense_feats, d_first_round)
    grad_bf = grad_scale * jnp.sum(d_first, axis=0)
    grads = jnp.swapaxes(grads.reshape(tables, replicas, share, columns), 0, 1)
    grads = grads.reshape(replicas * tables * share, columns)
    dense = (grad_wf, grad_bf, grad_ws, grad_bs, grad_vb, grad_ub, grad_bb)
    grads, dense = lax.optimization_barrier((grads, dense))
    grads = lax.psum_scatter(grads, "rep", scatter_dimension=0, tiled=True)
    dense_sums = lax.psum(dense, ("rep", "mp"))
    grads, dense_sums = lax.optimization_barrier((grads, dense_sums))
    grads = lax.psum_scatter(
        grads.astype(jnp.float32) * grad_scale, "mp", scatter_dimension=0, tiled=True
    )
    grads = lax.optimization_barrier(grads).astype(jnp.bfloat16)
    grads = lax.all_gather(grads, "rep", axis=0, tiled=True)
    return (
        cross_emb,
        cross_bot,
        grads[:, 2 * rank : 2 * rank + table_rows].T[None],
        grads[:, :rank],
        grads[:, rank : 2 * rank].T,
        grads[:, 2 * rank + table_rows],
        dense_sums[4].astype(jnp.bfloat16),
        dense_sums[5].astype(jnp.bfloat16),
        dense_sums[6].astype(jnp.bfloat16),
        dense_sums[0].astype(jnp.bfloat16),
        dense_sums[1].astype(jnp.bfloat16),
        dense_sums[2].astype(jnp.bfloat16),
        dense_sums[3].astype(jnp.bfloat16),
    )


def solution(mesh):
    return jax.shard_map(
        local,
        mesh=mesh,
        in_specs=(
            P(("rep", "mp"), None),
            P("rep", "mp", None),
            P("mp", None, None),
            P("mp", None),
            P(None, "mp"),
            P("mp"),
            P(),
            P(),
            P(),
            P(),
            P(),
            P(),
            P(),
            P(("rep", "mp"), None),
            P(("rep", "mp"), None),
        ),
        out_specs=(
            P(("rep", "mp"), None),
            P(("rep", "mp"), None),
            P("mp", None, None),
            P("mp", None),
            P(None, "mp"),
            P("mp"),
            P(),
            P(),
            P(),
            P(),
            P(),
            P(),
            P(),
        ),
        check_vma=False,
    )
```

profile of v0, /device:TPU:8, one launch (start us, length us, event | category | flops | bytes accessed | tf_op | source)
XLA Modules:
  0.0 810.7 jit_solution(15563284094259363290)
XLA Ops:
  7.3 1.1 copy.49
  10.1 1.0 concatenate.11
  11.2 57.4 %all_gather.9 = bf16[512,640]{1,0:T(8,128)(2,1)} all-gather(bf16[16,640]{1,0:T(8,128)(2,1)S(1)} %constant_dynamic-slice_fusion), channel_id=1, replica_groups=mesh['rep'=16,'mp'=32] {'mp'}, dimensions={0}, use_global_device_ids=true | all-gather | bytes 675840 | tf_op jit(solution)/shard_map/all_gather | solution.py:57
  68.5 1.3 convert_bitcast_fusion
  71.0 12.9 %all-to-all-start = ((bf16[32,64,128]{2,1,0:T(8,128)(2,1)}), bf16[32,64,128]{2,1,0:T(8,128)(2,1)S(1)}, u32[]{:S(2)}, u32[]{:S(2)}) async-start(bf16[32,64,128]{2,1,0:T(8,128)(2,1)} %bitcast.72), calls=%async_computation | async-start | bytes 1048576 | tf_op jit(solution)/shard_map/all_to_all | solution.py:63
  86.0 237.6 %all-gather.2.cloned.1.call-done = bf16[8192,640]{1,0:T(8,128)(2,1)} async-done(((bf16[512,640]{1,0:T(8,128)(2,1)}), bf16[8192,640]{1,0:T(8,128)(2,1)}) %all-gather.2.cloned.1.call-update) | async-done | bytes 10485776 | tf_op jit(solution)/shard_map/all_gather | solution.py:58
  323.5 9.6 %copy.52 = bf16[32,16,16,640]{3,2,1,0:T(8,128)(2,1)} copy(bf16[32,16,16,640]{3,2,0,1:T(8,128)(2,1)} %bitcast.87) | data formatting | bytes 20971520 | tf_op jit(solution)/shard_map/transpose | solution.py:59
  333.2 1.7 slice.32
  335.6 1.3 copy-done.4
  336.9 3.1 fusion.9
  340.0 3.1 copy.56
  343.1 3.0 convert_reduce_fusion
  346.2 3.7 fusion.5
  350.1 3.4 convolution_convert_fusion
  353.8 3.3 convolution_convert_fusion.1
  358.2 1.1 fusion.29
  359.3 1.4 convolution_multiply_fusion
  361.8 3.0 fusion.3
  364.8 1.5 fusion.1
  366.8 1.8 copy.58
  368.6 2.1 copy.61
  370.9 4.2 copy.62
  375.1 4.8 copy.60
  379.9 2.5 copy.59
  382.6 1.7 broadcast_in_dim.18
  384.3 18.8 %concatenate.14 = bf16[32,16,16,640]{3,2,0,1:T(8,128)(2,1)} concatenate(bf16[32,16,16,256]{3,2,0,1:T(8,128)(2,1)} %copy.59, bf16[32,16,16,256]{3,2,0,1:T(8,128)(2,1)} %copy.60, bf16[32,16,16,64]{3,2,0,1:T(8,128)(2,1)S(1)} %copy.61, bf16[32,16,16,1]{3,2,0,1:T(8,128)(2,1)} %copy.62, bf16[32,16,16,63]{3,2,0,1:T(8,128)(2,1)} %broadcast_in_dim.18), dimensions={3} | concatenate | bytes 20971520 | tf_op jit(solution)/shard_map/concatenate | solution.py:110
  403.2 1.1 copy-done.6
  404.4 125.4 %all-reduce.2 = (bf16[13,1024]{1,0:T(8,128)(2,1)}, bf16[1024]{0:T(1024)(128)(2,1)}, bf16[1024,256]{1,0:T(8,128)(2,1)}, bf16[256]{0:T(256)(128)(2,1)}, bf16[256,2...) all-reduce(f32[13,1024]{1,0:T(8,128)S(1)} %fusion.18, ...), channel_id=1, replica_groups=mesh['rep'=16,'mp'=32] {'rep','mp'}, use_global_device_ids=true, to_apply=%region_5.6 | all-reduce | flops 408064 | bytes 2448384 | tf_op jit(solution)/shard_map/psum | solution.py:137
  529.8 109.0 %reduce-scatter.3.cloned.1.call-done = bf16[512,640]{1,0:T(8,128)(2,1)} async-done(((bf16[8192,640]{1,0:T(8,128)(2,1)}), bf16[512,640]{1,0:T(8,128)(2,1)}) %reduce-scatter.3.cloned.1.call-update) | async-done | bytes 655376 | tf_op jit(solution)/shard_map/reduce_scatter | solution.py:136
  638.8 2.3 convert_multiply_fusion.3
  641.1 115.5 %reduce-scatter.5.cloned.1.call-done = f32[16,640]{1,0:T(8,128)} async-done(((f32[512,640]{1,0:T(8,128)}), f32[16,640]{1,0:T(8,128)}) %reduce-scatter.5.cloned.1.call-update) | async-done | bytes 40976 | tf_op jit(solution)/shard_map/reduce_scatter | solution.py:139
  757.3 44.0 %all_gather.11 = bf16[256,640]{1,0:T(8,128)(2,1)S(1)} all-gather(bf16[16,640]{1,0:T(8,128)(2,1)S(1)} %convert_element_type.164), channel_id=1, replica_groups=mesh['rep'=16,'mp'=32] {'rep'}, dimensions={0}, use_global_device_ids=true | all-gather | bytes 348160 | tf_op jit(solution)/shard_map/all_gather | solution.py:143
  (81 shorter events, 12.6 us)
Async XLA Ops:
  7.2 77.8 %copy-start = (bf16[1024,256]{1,0:T(8,128)(2,1)S(1)}, bf16[1024,256]{1,0:T(8,128)(2,1)}, u32[]{:S(2)}) copy-start(bf16[1024,256]{1,0:T(8,128)(2,1)} %param.26) | copy-start | bytes 1572868
  7.2 76.7 %copy-start.16 = (bf16[1024]{0:T(1024)(128)(2,1)S(1)}, bf16[1024]{0:T(1024)(128)(2,1)}, u32[]{:S(2)}) copy-start(bf16[1024]{0:T(1024)(128)(2,1)} %param.25) | copy-start | bytes 6148
  7.2 76.7 %copy-start.17 = (bf16[256]{0:T(256)(128)(2,1)S(1)}, bf16[256]{0:T(256)(128)(2,1)}, u32[]{:S(2)}) copy-start(bf16[256]{0:T(256)(128)(2,1)} %param.27) | copy-start | bytes 1540
  7.2 76.7 %copy-start.18 = (bf16[256]{0:T(256)(128)(2,1)S(1)}, bf16[256]{0:T(256)(128)(2,1)}, u32[]{:S(2)}) copy-start(bf16[256]{0:T(256)(128)(2,1)} %param.23) | copy-start | bytes 1540
  7.2 76.7 %copy-start.15 = (bf16[128,13]{0,1:T(8,128)(2,1)S(1)}, bf16[128,13]{0,1:T(8,128)(2,1)}, u32[]{:S(2)}) copy-start(bf16[128,13]{0,1:T(8,128)(2,1)} %param.15) | copy-start | bytes 9988
  7.2 76.7 %copy-start.14 = (bf16[13,1024]{1,0:T(8,128)(2,1)S(1)}, bf16[13,1024]{1,0:T(8,128)(2,1)}, u32[]{:S(2)}) copy-start(bf16[13,1024]{1,0:T(8,128)(2,1)} %param.24) | copy-start | bytes 79876
  7.2 77.8 %copy-start.11 = (bf16[128,256]{1,0:T(8,128)(2,1)S(1)}, bf16[128,256]{1,0:T(8,128)(2,1)}, u32[]{:S(2)}) copy-start(bf16[128,256]{1,0:T(8,128)(2,1)} %param.29) | copy-start | bytes 196612
  7.3 316.3 %all-gather.2.cloned.1.call-start = ((), (), s32[]{:S(2)}) async-start(), calls=%async_computation.3 | async-start | bytes 11141120 | tf_op jit(solution)/shard_map/all_gather | solution.py:58
  71.0 263.9 %all-to-all-start = ((bf16[32,64,128]{2,1,0:T(8,128)(2,1)}), bf16[32,64,128]{2,1,0:T(8,128)(2,1)S(1)}, u32[]{:S(2)}, u32[]{:S(2)}) async-start(bf16[32,64,128]{2,1,0:T(8,128)(2,1)} %bitcast.72), calls=%async_computation | async-start | bytes 1048576 | tf_op jit(solution)/shard_map/all_to_all | solution.py:63
  83.8 554.9 %reduce-scatter.3.cloned.1.call-start = ((), (), s32[]{:S(2)}) async-start(), calls=%async_computation.4 | async-start | bytes 11141120 | tf_op jit(solution)/shard_map/reduce_scatter | solution.py:136
  84.2 0.8 copy-start.9
  335.6 1.3 copy-start.4
  346.1 3.8 copy-start.13
  346.1 3.9 copy-start.2
  350.1 3.5 copy-start.8
  350.1 3.7 copy-start.5
  350.1 11.7 %slice-start = ((s8[10485760]{0:T(1024)(128)(4,1)}), s8[4194304]{0:T(1024)(128)(4,1)S(1)}, s32[]{:S(2)}) async-start(s8[10485760]{0:T(1024)(128)(4,1)} %bitcast.77), calls=%async_computation.6 | async-start | bytes 8388608
  350.1 11.7 %slice-start.1 = ((s8[10485760]{0:T(1024)(128)(4,1)}), s8[4194304]{0:T(1024)(128)(4,1)S(1)}, s32[]{:S(2)}) async-start(s8[10485760]{0:T(1024)(128)(4,1)} %bitcast.77), calls=%async_computation.7 | async-start | bytes 8388608
  353.8 4.1 copy-start.19
  353.8 4.4 copy-start.10
  353.8 8.0 slice-start.2
  375.1 4.8 copy-start.3
  379.9 2.5 copy-start.12
  403.1 1.2 copy-start.6
  403.1 1.3 copy-start.7
  403.2 401.0 %copy-start.1 = (bf16[1024,256]{1,0:T(8,128)(2,1)S(1)}, bf16[1024,256]{1,0:T(8,128)(2,1)}, u32[]{:S(2)}) copy-start(bf16[1024,256]{1,0:T(8,128)(2,1)} %param.26) | copy-start | bytes 1572868
  403.2 353.4 %reduce-scatter.5.cloned.1.call-start = ((), (), s32[]{:S(2)}) async-start(), calls=%async_computation.5 | async-start | bytes 1351680 | tf_op jit(solution)/shard_map/reduce_scatter | solution.py:139
Sparse Core Ops, SparseCore 0:
  68.7 254.8 all-gather.1
  403.3 235.4 reduce-scatter.2
  643.2 113.3 reduce-scatter.4
where the time goes:
time: 812 us; the launch traced here: 811 us
  waiting for transfers between devices  462 us (57%)
  blocking collectives  227 us (28%)
  local copies, waits for them, and re-layouts  61.7 us (8%)
  matrix products  25.6 us (3%)
  between operations  14.2 us (2%)
  starting transfers between devices  13 us (2%)
    all_gather x1, waiting for transfers between devices, local(): packed = lax.all_gather(packed, 'rep', axis=0, tiled=True)  238 us
    psum x1, blocking collectives, local(): dense_sums = lax.psum(dense, ('rep', 'mp'))  125 us
    reduce_scatter x1, waiting for transfers between devices, local(): lax.psum_scatter(grads.astype(jnp.float32) * grad_scale, 'mp', scatter_di...  115 us
    reduce_scatter x1, waiting for transfers between devices, local(): grads = lax.psum_scatter(grads, 'rep', scatter_dimension=0, tiled=True)  109 us
    all_gather x1, blocking collectives, local(): packed = lax.all_gather(packed, 'mp', axis=0, tiled=True)  57.4 us
    all_gather x1, blocking collectives, local(): grads = lax.all_gather(grads, 'rep', axis=0, tiled=True)  44 us
    concatenate x3, local copies, waits for them, and re-layouts, local(): jnp.concatenate([grad_v.astype(jnp.bfloat16), grad_u.astype(jnp.bfloat16)...  26.2 us
  transfers between devices with their start and end apart: 4, of which 3 were waited for; matrix products, arithmetic and copies ran while one was open for 2% of the time, Pallas kernels for 0%

commit v1 on v0

--- a/solution.py
+++ b/solution.py
@@ -134,7 +134,7 @@
     dense = (grad_wf, grad_bf, grad_ws, grad_bs, grad_vb, grad_ub, grad_bb)
     grads, dense = lax.optimization_barrier((grads, dense))
     grads = lax.psum_scatter(grads, "rep", scatter_dimension=0, tiled=True)
-    dense_sums = lax.psum(dense, ("rep", "mp"))
+    dense_sums = lax.psum(lax.psum(dense, "rep"), "mp")
     grads, dense_sums = lax.optimization_barrier((grads, dense_sums))
     grads = lax.psum_scatter(
         grads.astype(jnp.float32) * grad_scale, "mp", scatter_dimension=0, tiled=True

time: 812 us -> 1060 us (1.31)
  blocking collectives: 227 us -> 388 us
  waiting for transfers between devices: 462 us -> 546 us
    psum x1 -> x2, blocking collectives: 125 us -> 286 us  [local(): dense_sums = lax.psum(lax.psum(dense, 'rep'), 'mp')]
    psum x0 -> x1, waiting for transfers between devices: none -> 99.6 us  [local(): dense_sums = lax.psum(lax.psum(dense, 'rep'), 'mp')]
    reduce_scatter x1, waiting for transfers between devices: 109 us -> 30.4 us  [local(): grads = lax.psum_scatter(grads, 'rep', scatter_dimension=0, tiled=True)]
    reduce_scatter x1, waiting for transfers between devices: 115 us -> 177 us  [local(): lax.psum_scatter(grads.astype(jnp.float32) * grad_scale, 'mp', scatter_di...]
  transfers between devices with their start and end apart: 4 -> 5, of which waited for: 3 -> 4; matrix products, arithmetic and copies ran while one was open for 2% -> 1% of each run, Pallas kernels for 0% -> 0%
where the time goes in v1:
time: 1060 us
  waiting for transfers between devices  546 us (52%)
  blocking collectives  388 us (37%)
  local copies, waits for them, and re-layouts  60.3 us (6%)
  matrix products  32.1 us (3%)
  between operations  14.2 us (1%)
  starting transfers between devices  13 us (1%)
    psum x2, blocking collectives, local(): dense_sums = lax.psum(lax.psum(dense, 'rep'), 'mp')  286 us
    all_gather x1, waiting for transfers between devices, local(): packed = lax.all_gather(packed, 'rep', axis=0, tiled=True)  238 us
    reduce_scatter x1, waiting for transfers between devices, local(): lax.psum_scatter(grads.astype(jnp.float32) * grad_scale, 'mp', scatter_di...  177 us
    psum x1, waiting for transfers between devices, local(): dense_sums = lax.psum(lax.psum(dense, 'rep'), 'mp')  99.6 us
    all_gather x1, blocking collectives, local(): packed = lax.all_gather(packed, 'mp', axis=0, tiled=True)  57.4 us
    all_gather x1, blocking collectives, local(): grads = lax.all_gather(grads, 'rep', axis=0, tiled=True)  44.1 us
    reduce_scatter x1, waiting for transfers between devices, local(): grads = lax.psum_scatter(grads, 'rep', scatter_dimension=0, tiled=True)  30.4 us
    concatenate x3, local copies, waits for them, and re-layouts, local(): jnp.concatenate([grad_v.astype(jnp.bfloat16), grad_u.astype(jnp.bfloat16)...  26.2 us
  transfers between devices with their start and end apart: 5, of which 4 were waited for; matrix products, arithmetic and copies ran while one was open for 1% of the time, Pallas kernels for 0%

profile of v1, /device:TPU:8, one launch (start us, length us, event | category | flops | bytes accessed | tf_op | source)
XLA Modules:
  0.0 1060.4 jit_solution(10795764540435657977)
XLA Ops:
  7.3 1.1 copy.49
  11.2 57.4 %all_gather.9 = bf16[512,640]{1,0:T(8,128)(2,1)} all-gather(bf16[16,640]{1,0:T(8,128)(2,1)S(1)} %constant_dynamic-slice_fusion), channel_id=1, replica_groups=mesh['rep'=16,'mp'=32] {'mp'}, dimensions={0}, use_global_device_ids=true | all-gather | bytes 675840 | tf_op jit(solution)/shard_map/all_gather | solution.py:57
  68.5 1.3 convert_bitcast_fusion
  71.0 12.9 %all-to-all-start = ((bf16[32,64,128]{2,1,0:T(8,128)(2,1)}), bf16[32,64,128]{2,1,0:T(8,128)(2,1)S(1)}, u32[]{:S(2)}, u32[]{:S(2)}) async-start(bf16[32,64,128]{2,1,0:T(8,128)(2,1)} %bitcast.72), calls=%async_computation | async-start | bytes 1048576 | tf_op jit(solution)/shard_map/all_to_all | solution.py:63
  86.0 237.6 %all-gather.2.cloned.1.call-done = bf16[8192,640]{1,0:T(8,128)(2,1)} async-done(((bf16[512,640]{1,0:T(8,128)(2,1)}), bf16[8192,640]{1,0:T(8,128)(2,1)}) %all-gather.2.cloned.1.call-update) | async-done | bytes 10485776 | tf_op jit(solution)/shard_map/all_gather | solution.py:58
  323.5 9.6 copy.52
  333.1 1.7 slice.32
  335.6 1.3 copy-done.5
  336.9 3.8 fusion.9
  340.7 2.9 copy.56
  343.6 3.0 convert_reduce_fusion
  346.6 3.7 fusion.5
  350.6 3.3 convolution_convert_fusion
  354.1 3.3 convolution_convert_fusion.1
  358.4 1.1 fusion.29
  359.5 1.4 convolution_multiply_fusion
  362.7 6.0 fusion.3
  368.7 3.8 fusion.1
  373.0 1.8 copy.58
  374.8 2.1 copy.61
  377.1 4.2 copy.62
  381.3 4.8 copy.60
  386.1 2.5 copy.59
  388.7 1.7 broadcast_in_dim.18
  390.4 18.8 %concatenate.14 = bf16[32,16,16,640]{3,2,0,1:T(8,128)(2,1)} concatenate(bf16[32,16,16,256]{3,2,0,1:T(8,128)(2,1)} %copy.59, bf16[32,16,16,256]{3,2,0,1:T(8,128)(2,1)} %copy.60, bf16[32,16,16,64]{3,2,0,1:T(8,128)(2,1)S(1)} %copy.61, bf16[32,16,16,1]{3,2,0,1:T(8,128)(2,1)} %copy.62, bf16[32,16,16,63]{3,2,0,1:T(8,128)(2,1)} %broadcast_in_dim.18), dimensions={3} | concatenate | bytes 20971520 | tf_op jit(solution)/shard_map/concatenate | solution.py:110
  410.1 79.9 %all-reduce.1 = (f32[13,1024]{1,0:T(8,128)S(1)}, f32[1024]{0:T(1024)S(1)}, f32[256]{0:T(256)S(1)}, f32[256]{0:T(256)S(1)}) all-reduce(f32[13,1024]{1,0:T(8,128)S(1)} %fusion.18, f32[1024]{0:T(1024)S(1)} %broadcast_multiply_fusion, f32[256]{0:T(256)S(1)} %get-tuple-element.33, ...), channel_id=1, replica_groups=mesh['rep'=16,'mp'=32] {'rep'}, use_global_device_ids=true, to_apply=%region_5.6 | all-reduce | flops 14848 | bytes 118784 | tf_op jit(solution)/shard_map/psum | solution.py:137
  490.0 99.6 %all-reduce.6.cloned.1.call-done = (f32[1024,256]{1,0:T(8,128)}, f32[256,256]{1,0:T(8,128)}, f32[256,256]{1,0:T(8,128)}) async-done(((f32[1024,256]{1,0:T(8,128)}, f32[256,256]{1,0:T(8,128)}, f32[256,256]{1,0:T(8,128)}), (f32[1024,256]{1,0:T(8,128)}, f32[256,256]{1,0:T(8,128)}, f32[256,256]{1,0:T(8,128)})) %all-reduce.6.cloned.1.call-update) | async-done | bytes 1572880 | tf_op jit(solution)/shard_map/psum | solution.py:137
  589.6 206.5 %all-reduce.7 = (bf16[13,1024]{1,0:T(8,128)(2,1)}, bf16[1024]{0:T(1024)(128)(2,1)}, bf16[1024,256]{1,0:T(8,128)(2,1)}, bf16[256]{0:T(256)(128)(2,1)}, bf16[256,2...) all-reduce(f32[13,1024]{1,0:T(8,128)S(1)} %get-tuple-element.91, ...), channel_id=1, replica_groups=mesh['rep'=16,'mp'=32] {'mp'}, use_global_device_ids=true, to_apply=%region_6.7 | all-reduce | flops 408064 | bytes 2448384 | tf_op jit(solution)/shard_map/psum | solution.py:137
  796.1 30.4 %reduce-scatter.3.cloned.1.call-done = bf16[512,640]{1,0:T(8,128)(2,1)} async-done(((bf16[8192,640]{1,0:T(8,128)(2,1)}), bf16[512,640]{1,0:T(8,128)(2,1)}) %reduce-scatter.3.cloned.1.call-update) | async-done | bytes 655376 | tf_op jit(solution)/shard_map/reduce_scatter | solution.py:136
  826.4 2.3 convert_multiply_fusion.3
  828.7 177.4 %reduce-scatter.5.cloned.1.call-done = f32[16,640]{1,0:T(8,128)} async-done(((f32[512,640]{1,0:T(8,128)}), f32[16,640]{1,0:T(8,128)}) %reduce-scatter.5.cloned.1.call-update) | async-done | bytes 40976 | tf_op jit(solution)/shard_map/reduce_scatter | solution.py:139
  1006.9 44.1 %all_gather.11 = bf16[256,640]{1,0:T(8,128)(2,1)S(1)} all-gather(bf16[16,640]{1,0:T(8,128)(2,1)S(1)} %convert_element_type.164), channel_id=1, replica_groups=mesh['rep'=16,'mp'=32] {'rep'}, dimensions={0}, use_global_device_ids=true | all-gather | bytes 348160 | tf_op jit(solution)/shard_map/all_gather | solution.py:143
  (78 shorter events, 15.1 us)
Async XLA Ops:
  7.2 77.8 %copy-start = (bf16[1024,256]{1,0:T(8,128)(2,1)S(1)}, bf16[1024,256]{1,0:T(8,128)(2,1)}, u32[]{:S(2)}) copy-start(bf16[1024,256]{1,0:T(8,128)(2,1)} %param.26) | copy-start | bytes 1572868
  7.2 76.7 %copy-start.16 = (bf16[1024]{0:T(1024)(128)(2,1)S(1)}, bf16[1024]{0:T(1024)(128)(2,1)}, u32[]{:S(2)}) copy-start(bf16[1024]{0:T(1024)(128)(2,1)} %param.25) | copy-start | bytes 6148
  7.2 76.7 %copy-start.17 = (bf16[256]{0:T(256)(128)(2,1)S(1)}, bf16[256]{0:T(256)(128)(2,1)}, u32[]{:S(2)}) copy-start(bf16[256]{0:T(256)(128)(2,1)} %param.27) | copy-start | bytes 1540
  7.2 76.7 %copy-start.18 = (bf16[256]{0:T(256)(128)(2,1)S(1)}, bf16[256]{0:T(256)(128)(2,1)}, u32[]{:S(2)}) copy-start(bf16[256]{0:T(256)(128)(2,1)} %param.23) | copy-start | bytes 1540
  7.2 76.7 %copy-start.15 = (bf16[128,13]{0,1:T(8,128)(2,1)S(1)}, bf16[128,13]{0,1:T(8,128)(2,1)}, u32[]{:S(2)}) copy-start(bf16[128,13]{0,1:T(8,128)(2,1)} %param.15) | copy-start | bytes 9988
  7.2 76.7 %copy-start.14 = (bf16[13,1024]{1,0:T(8,128)(2,1)S(1)}, bf16[13,1024]{1,0:T(8,128)(2,1)}, u32[]{:S(2)}) copy-start(bf16[13,1024]{1,0:T(8,128)(2,1)} %param.24) | copy-start | bytes 79876
  7.2 77.8 %copy-start.10 = (bf16[128,256]{1,0:T(8,128)(2,1)S(1)}, bf16[128,256]{1,0:T(8,128)(2,1)}, u32[]{:S(2)}) copy-start(bf16[128,256]{1,0:T(8,128)(2,1)} %param.29) | copy-start | bytes 196612
  7.3 316.3 %all-gather.2.cloned.1.call-start = ((), (), s32[]{:S(2)}) async-start(), calls=%async_computation.3 | async-start | bytes 11141120 | tf_op jit(solution)/shard_map/all_gather | solution.py:58
  71.0 263.9 %all-to-all-start = ((bf16[32,64,128]{2,1,0:T(8,128)(2,1)}), bf16[32,64,128]{2,1,0:T(8,128)(2,1)S(1)}, u32[]{:S(2)}, u32[]{:S(2)}) async-start(bf16[32,64,128]{2,1,0:T(8,128)(2,1)} %bitcast.72), calls=%async_computation | async-start | bytes 1048576 | tf_op jit(solution)/shard_map/all_to_all | solution.py:63
  83.8 505.8 %all-reduce.6.cloned.1.call-start = ((), (), s32[]{:S(2)}) async-start(), calls=%async_computation.6 | async-start | bytes 3145728 | tf_op jit(solution)/shard_map/psum | solution.py:137
  84.2 0.8 copy-start.8
  335.6 1.3 copy-start.5
  346.6 3.8 copy-start.12
  346.6 3.8 copy-start.13
  346.6 3.9 copy-start.2
  350.6 3.3 copy-start.7
  350.6 3.5 copy-start.6
  354.1 4.1 copy-start.19
  354.1 4.3 copy-start.9
  362.7 6.0 copy-start.3
  381.3 4.8 copy-start.4
  386.1 2.5 copy-start.11
  409.3 417.1 %reduce-scatter.3.cloned.1.call-start = ((), (), s32[]{:S(2)}) async-start(), calls=%async_computation.4 | async-start | bytes 11141120 | tf_op jit(solution)/shard_map/reduce_scatter | solution.py:136
  410.1 643.8 %copy-start.1 = (bf16[1024,256]{1,0:T(8,128)(2,1)S(1)}, bf16[1024,256]{1,0:T(8,128)(2,1)}, u32[]{:S(2)}) copy-start(bf16[1024,256]{1,0:T(8,128)(2,1)} %param.26) | copy-start | bytes 1572868
  410.1 596.0 %reduce-scatter.5.cloned.1.call-start = ((), (), s32[]{:S(2)}) async-start(), calls=%async_computation.5 | async-start | bytes 1351680 | tf_op jit(solution)/shard_map/reduce_scatter | solution.py:139
Sparse Core Ops, SparseCore 0:
  68.7 254.8 all-gather.1
  409.4 180.1 all-reduce.5
  592.7 233.6 reduce-scatter.2
  831.3 174.7 reduce-scatter.4
